TPU v7x, 32 devices: a whole 2x2x4 slice. The times are simulated.
32 devices in a mesh: fx: 2 (over y), fy: 4 (over x, core), st: 4 (over z).
Axes of the slice: x: 2, y: 2, z: 4, core: 2. Of those that a mesh axis runs over, the one named last changes fastest.
Arguments:
- tangent_rhs: bfloat16 [4, 6, 64, 2, 4, 128], P('st', None, None, 'fx', 'fy'), may hold values from -6 to 6
- adjoint_rhs: bfloat16 [4, 6, 64, 2, 4, 128], P('st', None, None, 'fx', 'fy'), may hold values from -6 to 6
- jacobians: bfloat16 [3, 6, 6, 2, 4, 128], P(None, None, None, 'fx', 'fy'), may hold values from -0.75 to 0.75
- deriv: bfloat16 [3, 64, 64], replicated, may hold values from -0.75 to 0.75
- penalty: float32 [6], replicated, may hold values from 0.1 to 0.4
- second_order: float32 [6, 2, 4, 128], P(None, 'fx', 'fy'), may hold values from -4 to 4
- coupling: bfloat16 [6, 384], replicated, may hold values from -2.5 to 2.5
- shell_inverse: bfloat16 [16, 384, 384], P('st')
- shell_load: float32 [4, 16, 384], P(None, 'st'), may hold values from -6 to 6
- shell_adjoint_rhs: float32 [4, 16, 384], P(None, 'st'), may hold values from -6 to 6
- iface_elem: int32 [8, 128], P(('fx', 'fy')), may hold values from 0 to 127
- iface_node: int32 [8, 128], P(('fx', 'fy')), may hold values from 0 to 1023
- iface_weight: float32 [8, 128], P(('fx', 'fy')), may hold values from 0.5 to 2
- iface_count: int32 [8], P(('fx', 'fy')), may hold values from 0 to 128, as said below
Outputs:
- tangent_flow: bfloat16 [4, 6, 64, 2, 4, 128], P('st', None, None, 'fx', 'fy')
- adjoint_flow: bfloat16 [4, 6, 64, 2, 4, 128], P('st', None, None, 'fx', 'fy')
- shell_tangent: float32 [4, 16, 384], P(None, 'st')
- shell_adjoint: float32 [4, 16, 384], P(None, 'st')
Inputs may be any that keep to these rules, and one draw needn't show every extreme that they name: `iface_count`: at most 128 live slots in one flow block; some block has exactly 128.
All inputs are finite; a program needn't handle non-finite values.
Results may differ from a plain program's by a relative error of at most 0.0069.
Values may be sent and summed in bfloat16 or wider, within the bound.
No kernel may reach another device: no remote copies, remote signals or barrier semaphores. Data moves between devices by JAX's collectives and lax.ppermute only.
A program may use at most 64 MiB of HBM per device.

v0:
```python
import jax
import jax.numpy as jnp
from jax import lax
from jax.sharding import PartitionSpec as P

SDOF = 6
PN = 64
FSWEEP = 3
ROUNDS = 2
SIGMA = 0.5


def with_halo(value, sides, width):
    for axis, dim in sides:
        peers, length = (lax.axis_size(axis), value.shape[dim])
        up = [(i, (i + 1) % peers) for i in range(peers - 1)]
        down = [(j, i) for i, j in up]
        last = lax.slice_in_dim(value, length - width, length, axis=dim)
        initial = lax.slice_in_dim(value, 0, width, axis=dim)
        before = lax.ppermute(last, axis, up)
        after = lax.ppermute(initial, axis, down)
        value = jnp.concatenate([before, value, after], axis=dim)
    return value


def face_pair(lower_face, upper_face, below, above, axis):
    length = lower_face.shape[axis]
    beyond_upper = jnp.concatenate(
        [lax.slice_in_dim(lower_face, 1, length, axis=axis), above], axis=axis
    )
    beyond_lower = jnp.concatenate(
        [below, lax.slice_in_dim(upper_face, 0, length - 1, axis=axis)], axis=axis
    )
    return (lower_face - beyond_lower, upper_face - beyond_upper)


def place_faces(jump_low, jump_high, axis):
    middle_shape = list(jump_low.shape)
    middle_shape.insert(axis, 2)
    middle = jnp.zeros(middle_shape, jump_low.dtype)
    return jnp.concatenate(
        [jnp.expand_dims(jump_low, axis), middle, jnp.expand_dims(jump_high, axis)], axis=axis
    )


def as_cube(values):
    members, variables, points, size_x, size_y, size_z = values.shape
    return values.reshape(members, variables, 4, 4, 4, size_x, size_y, size_z)


def face_edges(values):
    cube = as_cube(values)
    received = []
    for node_axis in (2, 3):
        elem_axis = node_axis + 2
        lower_face = jnp.take(cube, 0, axis=node_axis)
        upper_face = jnp.take(cube, 3, axis=node_axis)
        edges = jnp.concatenate([lower_face, upper_face], axis=elem_axis)
        if node_axis == 2:
            extended = with_halo(edges, (("fx", 4),), 1)
        else:
            extended = with_halo(edges, (("fy", 5),), 1)
        below = lax.slice_in_dim(extended, 0, 1, axis=elem_axis)
        above = lax.slice_in_dim(extended, 3, 4, axis=elem_axis)
        received.append((below, above))
    return received


def flow_jumps(values, received):
    cube = as_cube(values)
    result = jnp.zeros(cube.shape, jnp.float32)
    for node_axis in (2, 3, 4):
        elem_axis = node_axis + 2
        lower_face = jnp.take(cube, 0, axis=node_axis).astype(jnp.float32)
        upper_face = jnp.take(cube, 3, axis=node_axis).astype(jnp.float32)
        if received is None or node_axis == 4:
            below = jnp.zeros_like(lax.slice_in_dim(lower_face, 0, 1, axis=elem_axis))
            above = below
        else:
            below = received[node_axis - 2][0].astype(jnp.float32)
            above = received[node_axis - 2][1].astype(jnp.float32)
        jump_low, jump_high = face_pair(lower_face, upper_face, below, above, elem_axis)
        result = result + place_faces(jump_low, jump_high, node_axis)
    return result.reshape(values.shape)


def volume(values, deriv_mats, jac_mats):
    grads = jnp.einsum("kpq,vqxyz->kvpxyz", deriv_mats, values, preferred_element_type=jnp.float32)
    result = jnp.sum(jac_mats[0][:, :, None] * grads[0][None], axis=1)
    for axis_index in (1, 2):
        result = result + jnp.sum(
            jac_mats[axis_index][:, :, None] * grads[axis_index][None], axis=1
        )
    return result


def operator(states, operator_kinds, penalty):
    values = lax.optimization_barrier(states.astype(jnp.bfloat16))
    received = face_edges(values)
    jumps = flow_jumps(values, received)
    volumes = jnp.stack(
        [
            volume(values[member], operator_kinds[member][0], operator_kinds[member][1])
            for member in range(len(operator_kinds))
        ]
    )
    return states + volumes + penalty[None, :, None, None, None, None] * jumps


def body(
    tangent_rhs,
    adjoint_rhs,
    jacobians,
    deriv,
    penalty,
    second_order,
    coupling,
    shell_inverse,
    shell_load,
    shell_adjoint_rhs,
    iface_elem,
    iface_node,
    iface_weight,
    iface_count,
):
    state_shape = tangent_rhs.shape
    variables = state_shape[1]
    points = state_shape[2]
    elements = state_shape[3] * state_shape[4] * state_shape[5]
    slots = iface_elem.shape[1]
    live = (jnp.arange(slots, dtype=jnp.int32) < iface_count[0]).astype(jnp.float32)
    weights = iface_weight[0] * live
    elem_index = iface_elem[0]
    node_index = iface_node[0]
    dof_rows = jnp.arange(SDOF, dtype=jnp.int32)[:, None]
    columns = (node_index // PN)[None, :] * (SDOF * PN) + dof_rows * PN + (node_index % PN)[None, :]
    forward_jac = jacobians.astype(jnp.float32)
    forward_kind = (deriv, forward_jac)
    backward_kind = (jnp.swapaxes(deriv, 1, 2), jnp.swapaxes(forward_jac, 1, 2))
    coupling_cols = coupling.T

    def shell_solve(rhs):
        return jnp.einsum(
            "pab,dpb->dpa",
            shell_inverse,
            rhs.astype(jnp.bfloat16),
            preferred_element_type=jnp.float32,
        )

    shell_tangent = shell_solve(shell_load)
    shell_adjoint = jnp.zeros(shell_load.shape, jnp.float32)
    tangent = jnp.zeros(state_shape, jnp.float32)
    adjoint = jnp.zeros(state_shape, jnp.float32)
    for round_index in range(ROUNDS):
        received = lax.all_to_all(
            shell_tangent.astype(jnp.bfloat16), "st", split_axis=0, concat_axis=1, tiled=True
        )
        picked = received.reshape(-1)[columns]
        pushed_cols = (
            jnp.dot(coupling_cols, picked, preferred_element_type=jnp.float32) * weights[None, :]
        )
        pushed = (
            jnp.zeros((variables * points, elements), jnp.float32)
            .at[:, elem_index]
            .add(pushed_cols)
        )
        force = tangent_rhs.astype(jnp.float32) - pushed.reshape(state_shape)
        adjoint_source = adjoint_rhs.astype(jnp.float32) + second_order[None, :, None] * tangent
        paired = jnp.concatenate([tangent, adjoint])
        sources = jnp.concatenate([force, adjoint_source])
        for sweep in range(FSWEEP):
            paired = paired + SIGMA * (
                sources - operator(paired, (forward_kind, backward_kind), penalty)
            )
        tangent = paired[:1]
        adjoint = paired[1:]
        adjoint_values = adjoint.astype(jnp.bfloat16).reshape(variables * points, elements)
        gathered = adjoint_values[:, elem_index]
        loads = jnp.dot(coupling, gathered, preferred_element_type=jnp.float32) * weights[None, :]
        panels = received.shape[1]
        partial_loads = jnp.zeros((panels * SDOF * PN,), jnp.float32).at[columns].add(loads)
        partial_loads = partial_loads.reshape(1, panels, SDOF * PN)
        summed = lax.psum(partial_loads, ("fx", "fy"))
        owned = lax.all_to_all(summed, "st", split_axis=1, concat_axis=0, tiled=True)
        shell_adjoint = shell_solve(shell_adjoint_rhs - owned)
        shell_tangent = shell_solve(shell_load + shell_adjoint)
    return (
        tangent.astype(jnp.bfloat16),
        adjoint.astype(jnp.bfloat16),
        shell_tangent,
        shell_adjoint,
    )


def solution(mesh):
    in_specs = (
        P("st", None, None, "fx", "fy", None),
        P("st", None, None, "fx", "fy", None),
        P(None, None, None, "fx", "fy", None),
        P(),
        P(),
        P(None, "fx", "fy", None),
        P(),
        P("st", None, None),
        P(None, "st", None),
        P(None, "st", None),
        P(("fx", "fy"), None),
        P(("fx", "fy"), None),
        P(("fx", "fy"), None),
        P(("fx", "fy")),
    )
    out_specs = (
        P("st", None, None, "fx", "fy", None),
        P("st", None, None, "fx", "fy", None),
        P(None, "st", None),
        P(None, "st", None),
    )
    return jax.shard_map(body, mesh=mesh, in_specs=in_specs, out_specs=out_specs, check_vma=False)
```

profile of v0, /device:TPU:0, one launch (start us, length us, event | category | flops | bytes accessed | tf_op | source)
XLA Modules:
  0.0 207.5 jit_solution(6584082621477791752)
XLA Ops:
  0.7 5.0 %collective-permute-start = (bf16[2,6,4,4,1,1,128]{6,3,2,1,0,5,4:T(4,128)(2,1)S(1)}, bf16[2,6,4,4,1,1,128]{6,3,2,1,0,5,4:T(4,128)(2,1)S(1)}, u32[]{:S(2)}, u32[]{:S(2)}) collective-permute-start(bf16[2,6,4,4,1,1,128]{6,3,2,1,0,5,4:T(4,128)(2,1)S(1)} %get-tuple-element.197), channel_id=1, source_target_pairs={{0,16},{1,17},{2,18},{3,19},{4,20},{5,21},{6,22},{7,23},{8,24},{9,... | collective-permute-start | bytes 147464 | tf_op jit(solution)/shard_map/ppermute | solution.py:20
  11.7 4.9 %all-to-all-start = ((bf16[4,4,384]{2,1,0:T(4,128)(2,1)}), bf16[4,4,384]{2,1,0:T(4,128)(2,1)S(1)}, u32[]{:S(2)}, u32[]{:S(2)}) async-start(bf16[4,4,384]{2,1,0:T(4,128)(2,1)} %copy.260), calls=%async_computation | async-start | bytes 24576 | tf_op jit(solution)/shard_map/all_to_all | solution.py:155
  22.2 5.0 %gather_fusion = bf16[768]{0:T(1024)(128)(2,1)S(1)} fusion(bf16[6144]{0:T(1024)(128)(2,1)S(1)} %reshape.2599, s32[1024]{0:T(1024)S(1)} %pad_clamp_fusion.1), kind=kCustom, calls=%fused_computation | custom fusion | bytes 6144 | tf_op jit(solution)/shard_map/gather | solution.py:158
  31.5 4.4 %collective-permute-start.4 = (bf16[2,6,4,4,1,1,128]{6,3,2,1,0,5,4:T(4,128)(2,1)S(1)}, bf16[2,6,4,4,1,1,128]{6,3,2,1,0,5,4:T(4,128)(2,1)S(1)}, u32[]{:S(2)}, u32[]{:S(2)}) collective-permute-start(bf16[2,6,4,4,1,1,128]{6,3,2,1,0,5,4:T(4,128)(2,1)S(1)} %get-tuple-element.187), channel_id=1, source_target_pairs={{0,16},{1,17},{2,18},{3,19},{4,20},{5,21},{6,22},{7,23},{8,24},{9,... | collective-permute-start | bytes 147464 | tf_op jit(solution)/shard_map/ppermute | solution.py:20
  37.2 3.0 %collective-permute-start.6 = (bf16[2,6,4,4,1,1,128]{6,3,2,1,0,5,4:T(4,128)(2,1)S(1)}, bf16[2,6,4,4,1,1,128]{6,3,2,1,0,5,4:T(4,128)(2,1)S(1)}, u32[]{:S(2)}, u32[]{:S(2)}) collective-permute-start(bf16[2,6,4,4,1,1,128]{6,3,2,1,0,5,4:T(4,128)(2,1)S(1)} %get-tuple-element.185), channel_id=1, source_target_pairs={{0,4},{4,8},{8,12},{1,5},{5,9},{9,13},{2,6},{6,10},{10,14},{3,7},{... | collective-permute-start | bytes 147464 | tf_op jit(solution)/shard_map/ppermute | solution.py:20
  42.3 4.1 %collective-permute-done.7 = bf16[2,6,4,4,1,1,128]{6,3,2,1,0,5,4:T(4,128)(2,1)S(1)} collective-permute-done((bf16[2,6,4,4,1,1,128]{6,3,2,1,0,5,4:T(4,128)(2,1)S(1)}, bf16[2,6,4,4,1,1,128]{6,3,2,1,0,5,4:T(4,128)(2,1)S(1)}, u32[]{:S(2)}, u32[]{:S(2)}) %collective-permute-start.7) | collective-permute-done | bytes 49184 | tf_op jit(solution)/shard_map/ppermute | solution.py:21
  48.7 4.7 %collective-permute-start.10 = (bf16[2,6,4,4,1,1,128]{6,3,2,1,0,5,4:T(4,128)(2,1)S(1)}, bf16[2,6,4,4,1,1,128]{6,3,2,1,0,5,4:T(4,128)(2,1)S(1)}, u32[]{:S(2)}, u32[]{:S(2)}) collective-permute-start(bf16[2,6,4,4,1,1,128]{6,3,2,1,0,5,4:T(4,128)(2,1)S(1)} %get-tuple-element.175), channel_id=1, source_target_pairs={{0,4},{4,8},{8,12},{1,5},{5,9},{9,13},{2,6},{6,10},{10,14},{3,7},{... | collective-permute-start | bytes 147464 | tf_op jit(solution)/shard_map/ppermute | solution.py:20
  54.7 4.5 %collective-permute-start.8 = (bf16[2,6,4,4,1,1,128]{6,3,2,1,0,5,4:T(4,128)(2,1)S(1)}, bf16[2,6,4,4,1,1,128]{6,3,2,1,0,5,4:T(4,128)(2,1)S(1)}, u32[]{:S(2)}, u32[]{:S(2)}) collective-permute-start(bf16[2,6,4,4,1,1,128]{6,3,2,1,0,5,4:T(4,128)(2,1)S(1)} %get-tuple-element.177), channel_id=1, source_target_pairs={{0,16},{1,17},{2,18},{3,19},{4,20},{5,21},{6,22},{7,23},{8,24},{9,... | collective-permute-start | bytes 147464 | tf_op jit(solution)/shard_map/ppermute | solution.py:20
  61.2 4.4 %collective-permute-done.9 = bf16[2,6,4,4,1,1,128]{6,3,2,1,0,5,4:T(4,128)(2,1)S(1)} collective-permute-done((bf16[2,6,4,4,1,1,128]{6,3,2,1,0,5,4:T(4,128)(2,1)S(1)}, bf16[2,6,4,4,1,1,128]{6,3,2,1,0,5,4:T(4,128)(2,1)S(1)}, u32[]{:S(2)}, u32[]{:S(2)}) %collective-permute-start.9) | collective-permute-done | bytes 49184 | tf_op jit(solution)/shard_map/ppermute | solution.py:21
  71.2 2.1 collective-permute-start.12
  75.3 4.8 %scatter_custom_fusion.1 = f32[6144]{0:T(1024)S(1)} fusion(s32[768]{0:T(1024)} %copy-done.12, f32[768]{0:T(1024)S(1)} %fusion.5, f32[]{:T(128)} %constant.129.clone.1), kind=kCustom, calls=%fused_computation.296 | custom fusion | flops 768 | bytes 25088 | tf_op jit(solution)/shard_map/scatter-add | solution.py:181
  80.0 23.1 %psum.14 = f32[1,16,384]{2,0,1:T(1,128)} all-reduce(f32[1,16,384]{2,0,1:T(1,128)S(1)} %bitcast.739), channel_id=1, replica_groups=mesh['fx'=2,'fy'=4,'st'=4] {'fx','fy'}, use_global_device_ids=true, to_apply=%region_20.27 | all-reduce | flops 6144 | bytes 49152 | tf_op jit(solution)/shard_map/psum | solution.py:183
  103.2 3.9 %all-to-all-start.1 = ((f32[1,16,384]{2,0,1:T(1,128)}), f32[1,16,384]{2,0,1:T(1,128)}, u32[]{:S(2)}, u32[]{:S(2)}) async-start(f32[1,16,384]{2,0,1:T(1,128)} %psum.14), calls=%async_computation.1 | async-start | bytes 49152 | tf_op jit(solution)/shard_map/all_to_all | solution.py:184
  117.6 5.1 %all-to-all-start.2 = ((bf16[4,4,384]{2,1,0:T(4,128)(2,1)}), bf16[4,4,384]{2,1,0:T(4,128)(2,1)S(1)}, u32[]{:S(2)}, u32[]{:S(2)}) async-start(bf16[4,4,384]{2,1,0:T(4,128)(2,1)} %copy.301), calls=%async_computation.2 | async-start | bytes 24576 | tf_op jit(solution)/shard_map/all_to_all | solution.py:155
  123.9 4.4 %all-to-all-done.2 = bf16[4,4,384]{2,1,0:T(4,128)(2,1)S(1)} async-done(((bf16[4,4,384]{2,1,0:T(4,128)(2,1)}), bf16[4,4,384]{2,1,0:T(4,128)(2,1)S(1)}, u32[]{:S(2)}, u32[]{:S(2)}) %all-to-all-start.2) | async-done | bytes 12320 | tf_op jit(solution)/shard_map/all_to_all | solution.py:155
  128.3 5.0 %gather_fusion.2 = bf16[768]{0:T(1024)(128)(2,1)S(1)} fusion(bf16[6144]{0:T(1024)(128)(2,1)S(1)} %reshape.2612, s32[1024]{0:T(1024)S(1)} %pad_clamp_fusion.1), kind=kCustom, calls=%fused_computation.2 | custom fusion | bytes 6144 | tf_op jit(solution)/shard_map/gather | solution.py:158
  137.1 4.5 %collective-permute-start.16 = (bf16[2,6,4,4,1,1,128]{6,3,2,1,0,5,4:T(4,128)(2,1)S(1)}, bf16[2,6,4,4,1,1,128]{6,3,2,1,0,5,4:T(4,128)(2,1)S(1)}, u32[]{:S(2)}, u32[]{:S(2)}) collective-permute-start(bf16[2,6,4,4,1,1,128]{6,3,2,1,0,5,4:T(4,128)(2,1)S(1)} %get-tuple-element.157), channel_id=1, source_target_pairs={{0,16},{1,17},{2,18},{3,19},{4,20},{5,21},{6,22},{7,23},{8,24},{9,... | collective-permute-start | bytes 147464 | tf_op jit(solution)/shard_map/ppermute | solution.py:20
  145.7 1.9 collective-permute-done.17
  147.6 1.9 collective-permute-done.19
  151.2 4.5 %collective-permute-start.20 = (bf16[2,6,4,4,1,1,128]{6,3,2,1,0,5,4:T(4,128)(2,1)S(1)}, bf16[2,6,4,4,1,1,128]{6,3,2,1,0,5,4:T(4,128)(2,1)S(1)}, u32[]{:S(2)}, u32[]{:S(2)}) collective-permute-start(bf16[2,6,4,4,1,1,128]{6,3,2,1,0,5,4:T(4,128)(2,1)S(1)} %get-tuple-element.147), channel_id=1, source_target_pairs={{0,16},{1,17},{2,18},{3,19},{4,20},{5,21},{6,22},{7,23},{8,24},{9,... | collective-permute-start | bytes 147464 | tf_op jit(solution)/shard_map/ppermute | solution.py:20
  157.0 4.4 %collective-permute-start.22 = (bf16[2,6,4,4,1,1,128]{6,3,2,1,0,5,4:T(4,128)(2,1)S(1)}, bf16[2,6,4,4,1,1,128]{6,3,2,1,0,5,4:T(4,128)(2,1)S(1)}, u32[]{:S(2)}, u32[]{:S(2)}) collective-permute-start(bf16[2,6,4,4,1,1,128]{6,3,2,1,0,5,4:T(4,128)(2,1)S(1)} %get-tuple-element.145), channel_id=1, source_target_pairs={{0,4},{4,8},{8,12},{1,5},{5,9},{9,13},{2,6},{6,10},{10,14},{3,7},{... | collective-permute-start | bytes 147464 | tf_op jit(solution)/shard_map/ppermute | solution.py:20
  167.3 4.8 %scatter_custom_fusion.3 = f32[6144]{0:T(1024)S(1)} fusion(s32[768]{0:T(1024)} %copy-done.12, f32[768]{0:T(1024)S(1)} %fusion.4, f32[]{:T(128)} %constant.129.clone.1), kind=kCustom, calls=%fused_computation.294 | custom fusion | flops 768 | bytes 25088 | tf_op jit(solution)/shard_map/scatter-add | solution.py:181
  172.0 25.3 %psum.15 = f32[1,16,384]{2,0,1:T(1,128)S(1)} all-reduce(f32[1,16,384]{2,0,1:T(1,128)S(1)} %bitcast.738), channel_id=1, replica_groups=mesh['fx'=2,'fy'=4,'st'=4] {'fx','fy'}, use_global_device_ids=true, to_apply=%region_41.48 | all-reduce | flops 6144 | bytes 49152 | tf_op jit(solution)/shard_map/psum | solution.py:183
  197.3 8.0 %all_to_all.42 = f32[1,16,384]{2,0,1:T(1,128)S(1)} all-to-all(f32[1,16,384]{2,0,1:T(1,128)S(1)} %psum.15), channel_id=1, replica_groups=mesh['fx'=2,'fy'=4,'st'=4] {'st'}, dimensions={1} | all-to-all | bytes 49152 | tf_op jit(solution)/shard_map/all_to_all | solution.py:184
  (264 shorter events, 60.9 us)
Async XLA Ops:
  0.7 28.4 %collective-permute-start = (bf16[2,6,4,4,1,1,128]{6,3,2,1,0,5,4:T(4,128)(2,1)S(1)}, bf16[2,6,4,4,1,1,128]{6,3,2,1,0,5,4:T(4,128)(2,1)S(1)}, u32[]{:S(2)}, u32[]{:S(2)}) collective-permute-start(bf16[2,6,4,4,1,1,128]{6,3,2,1,0,5,4:T(4,128)(2,1)S(1)} %get-tuple-element.197), channel_id=1, source_target_pairs={{0,16},{1,17},{2,18},{3,19},{4,20},{5,21},{6,22},{7,23},{8,24},{9,... | collective-permute-start | bytes 147464 | tf_op jit(solution)/shard_map/ppermute | solution.py:20
  5.8 23.3 %collective-permute-start.1 = (bf16[2,6,4,4,1,1,128]{6,3,2,1,0,5,4:T(4,128)(2,1)S(1)}, bf16[2,6,4,4,1,1,128]{6,3,2,1,0,5,4:T(4,128)(2,1)S(1)}, u32[]{:S(2)}, u32[]{:S(2)}) collective-permute-start(bf16[2,6,4,4,1,1,128]{6,3,2,1,0,5,4:T(4,128)(2,1)S(1)} %get-tuple-element.198), channel_id=1, source_target_pairs={{16,0},{17,1},{18,2},{19,3},{20,4},{21,5},{22,6},{23,7},{24,8},{25... | collective-permute-start | bytes 147464 | tf_op jit(solution)/shard_map/ppermute | solution.py:21
  7.1 22.0 %collective-permute-start.2 = (bf16[2,6,4,4,1,1,128]{6,3,2,1,0,5,4:T(4,128)(2,1)S(1)}, bf16[2,6,4,4,1,1,128]{6,3,2,1,0,5,4:T(4,128)(2,1)S(1)}, u32[]{:S(2)}, u32[]{:S(2)}) collective-permute-start(bf16[2,6,4,4,1,1,128]{6,3,2,1,0,5,4:T(4,128)(2,1)S(1)} %get-tuple-element.195), channel_id=1, source_target_pairs={{0,4},{4,8},{8,12},{1,5},{5,9},{9,13},{2,6},{6,10},{10,14},{3,7},{... | collective-permute-start | bytes 147464 | tf_op jit(solution)/shard_map/ppermute | solution.py:20
  8.6 20.5 %collective-permute-start.3 = (bf16[2,6,4,4,1,1,128]{6,3,2,1,0,5,4:T(4,128)(2,1)S(1)}, bf16[2,6,4,4,1,1,128]{6,3,2,1,0,5,4:T(4,128)(2,1)S(1)}, u32[]{:S(2)}, u32[]{:S(2)}) collective-permute-start(bf16[2,6,4,4,1,1,128]{6,3,2,1,0,5,4:T(4,128)(2,1)S(1)} %get-tuple-element.196), channel_id=1, source_target_pairs={{4,0},{8,4},{12,8},{5,1},{9,5},{13,9},{6,2},{10,6},{14,10},{7,3},{... | collective-permute-start | bytes 147464 | tf_op jit(solution)/shard_map/ppermute | solution.py:21
  11.7 10.5 %all-to-all-start = ((bf16[4,4,384]{2,1,0:T(4,128)(2,1)}), bf16[4,4,384]{2,1,0:T(4,128)(2,1)S(1)}, u32[]{:S(2)}, u32[]{:S(2)}) async-start(bf16[4,4,384]{2,1,0:T(4,128)(2,1)} %copy.260), calls=%async_computation | async-start | bytes 24576 | tf_op jit(solution)/shard_map/all_to_all | solution.py:155
  31.5 10.2 %collective-permute-start.4 = (bf16[2,6,4,4,1,1,128]{6,3,2,1,0,5,4:T(4,128)(2,1)S(1)}, bf16[2,6,4,4,1,1,128]{6,3,2,1,0,5,4:T(4,128)(2,1)S(1)}, u32[]{:S(2)}, u32[]{:S(2)}) collective-permute-start(bf16[2,6,4,4,1,1,128]{6,3,2,1,0,5,4:T(4,128)(2,1)S(1)} %get-tuple-element.187), channel_id=1, source_target_pairs={{0,16},{1,17},{2,18},{3,19},{4,20},{5,21},{6,22},{7,23},{8,24},{9,... | collective-permute-start | bytes 147464 | tf_op jit(solution)/shard_map/ppermute | solution.py:20
  35.9 6.3 %collective-permute-start.5 = (bf16[2,6,4,4,1,1,128]{6,3,2,1,0,5,4:T(4,128)(2,1)S(1)}, bf16[2,6,4,4,1,1,128]{6,3,2,1,0,5,4:T(4,128)(2,1)S(1)}, u32[]{:S(2)}, u32[]{:S(2)}) collective-permute-start(bf16[2,6,4,4,1,1,128]{6,3,2,1,0,5,4:T(4,128)(2,1)S(1)} %get-tuple-element.188), channel_id=1, source_target_pairs={{16,0},{17,1},{18,2},{19,3},{20,4},{21,5},{22,6},{23,7},{24,8},{25... | collective-permute-start | bytes 147464 | tf_op jit(solution)/shard_map/ppermute | solution.py:21
  40.3 6.1 %collective-permute-start.7 = (bf16[2,6,4,4,1,1,128]{6,3,2,1,0,5,4:T(4,128)(2,1)S(1)}, bf16[2,6,4,4,1,1,128]{6,3,2,1,0,5,4:T(4,128)(2,1)S(1)}, u32[]{:S(2)}, u32[]{:S(2)}) collective-permute-start(bf16[2,6,4,4,1,1,128]{6,3,2,1,0,5,4:T(4,128)(2,1)S(1)} %get-tuple-element.186), channel_id=1, source_target_pairs={{4,0},{8,4},{12,8},{5,1},{9,5},{13,9},{6,2},{10,6},{14,10},{7,3},{... | collective-permute-start | bytes 147464 | tf_op jit(solution)/shard_map/ppermute | solution.py:21
  48.7 12.0 %collective-permute-start.10 = (bf16[2,6,4,4,1,1,128]{6,3,2,1,0,5,4:T(4,128)(2,1)S(1)}, bf16[2,6,4,4,1,1,128]{6,3,2,1,0,5,4:T(4,128)(2,1)S(1)}, u32[]{:S(2)}, u32[]{:S(2)}) collective-permute-start(bf16[2,6,4,4,1,1,128]{6,3,2,1,0,5,4:T(4,128)(2,1)S(1)} %get-tuple-element.175), channel_id=1, source_target_pairs={{0,4},{4,8},{8,12},{1,5},{5,9},{9,13},{2,6},{6,10},{10,14},{3,7},{... | collective-permute-start | bytes 147464 | tf_op jit(solution)/shard_map/ppermute | solution.py:20
  53.4 7.3 %collective-permute-start.11 = (bf16[2,6,4,4,1,1,128]{6,3,2,1,0,5,4:T(4,128)(2,1)S(1)}, bf16[2,6,4,4,1,1,128]{6,3,2,1,0,5,4:T(4,128)(2,1)S(1)}, u32[]{:S(2)}, u32[]{:S(2)}) collective-permute-start(bf16[2,6,4,4,1,1,128]{6,3,2,1,0,5,4:T(4,128)(2,1)S(1)} %get-tuple-element.176), channel_id=1, source_target_pairs={{4,0},{8,4},{12,8},{5,1},{9,5},{13,9},{6,2},{10,6},{14,10},{7,3},{... | collective-permute-start | bytes 147464 | tf_op jit(solution)/shard_map/ppermute | solution.py:21
  54.7 6.5 %collective-permute-start.8 = (bf16[2,6,4,4,1,1,128]{6,3,2,1,0,5,4:T(4,128)(2,1)S(1)}, bf16[2,6,4,4,1,1,128]{6,3,2,1,0,5,4:T(4,128)(2,1)S(1)}, u32[]{:S(2)}, u32[]{:S(2)}) collective-permute-start(bf16[2,6,4,4,1,1,128]{6,3,2,1,0,5,4:T(4,128)(2,1)S(1)} %get-tuple-element.177), channel_id=1, source_target_pairs={{0,16},{1,17},{2,18},{3,19},{4,20},{5,21},{6,22},{7,23},{8,24},{9,... | collective-permute-start | bytes 147464 | tf_op jit(solution)/shard_map/ppermute | solution.py:20
  59.3 6.4 %collective-permute-start.9 = (bf16[2,6,4,4,1,1,128]{6,3,2,1,0,5,4:T(4,128)(2,1)S(1)}, bf16[2,6,4,4,1,1,128]{6,3,2,1,0,5,4:T(4,128)(2,1)S(1)}, u32[]{:S(2)}, u32[]{:S(2)}) collective-permute-start(bf16[2,6,4,4,1,1,128]{6,3,2,1,0,5,4:T(4,128)(2,1)S(1)} %get-tuple-element.178), channel_id=1, source_target_pairs={{16,0},{17,1},{18,2},{19,3},{20,4},{21,5},{22,6},{23,7},{24,8},{25... | collective-permute-start | bytes 147464 | tf_op jit(solution)/shard_map/ppermute | solution.py:21
  71.2 51.5 %collective-permute-start.12 = (bf16[2,6,4,4,1,1,128]{6,3,2,1,0,5,4:T(4,128)(2,1)}, bf16[2,6,4,4,1,1,128]{6,3,2,1,0,5,4:T(4,128)(2,1)}, u32[]{:S(2)}, u32[]{:S(2)}) collective-permute-start(bf16[2,6,4,4,1,1,128]{6,3,2,1,0,5,4:T(4,128)(2,1)} %get-tuple-element.167), channel_id=1, source_target_pairs={{0,16},{1,17},{2,18},{3,19},{4,20},{5,21},{6,22},{7,23},{8,24},{9,... | collective-permute-start | bytes 147464 | tf_op jit(solution)/shard_map/ppermute | solution.py:20
  103.2 10.7 %all-to-all-start.1 = ((f32[1,16,384]{2,0,1:T(1,128)}), f32[1,16,384]{2,0,1:T(1,128)}, u32[]{:S(2)}, u32[]{:S(2)}) async-start(f32[1,16,384]{2,0,1:T(1,128)} %psum.14), calls=%async_computation.1 | async-start | bytes 49152 | tf_op jit(solution)/shard_map/all_to_all | solution.py:184
  110.0 12.7 %collective-permute-start.13 = (bf16[2,6,4,4,1,1,128]{6,3,2,1,0,5,4:T(4,128)(2,1)}, bf16[2,6,4,4,1,1,128]{6,3,2,1,0,5,4:T(4,128)(2,1)S(1)}, u32[]{:S(2)}, u32[]{:S(2)}) collective-permute-start(bf16[2,6,4,4,1,1,128]{6,3,2,1,0,5,4:T(4,128)(2,1)} %get-tuple-element.168), channel_id=1, source_target_pairs={{16,0},{17,1},{18,2},{19,3},{20,4},{21,5},{22,6},{23,7},{24,8},{25... | collective-permute-start | bytes 147464 | tf_op jit(solution)/shard_map/ppermute | solution.py:21
  111.3 11.4 %collective-permute-start.14 = (bf16[2,6,4,4,1,1,128]{6,3,2,1,0,5,4:T(4,128)(2,1)}, bf16[2,6,4,4,1,1,128]{6,3,2,1,0,5,4:T(4,128)(2,1)S(1)}, u32[]{:S(2)}, u32[]{:S(2)}) collective-permute-start(bf16[2,6,4,4,1,1,128]{6,3,2,1,0,5,4:T(4,128)(2,1)} %get-tuple-element.165), channel_id=1, source_target_pairs={{0,4},{4,8},{8,12},{1,5},{5,9},{9,13},{2,6},{6,10},{10,14},{3,7},{... | collective-permute-start | bytes 147464 | tf_op jit(solution)/shard_map/ppermute | solution.py:20
  112.6 10.1 %collective-permute-start.15 = (bf16[2,6,4,4,1,1,128]{6,3,2,1,0,5,4:T(4,128)(2,1)}, bf16[2,6,4,4,1,1,128]{6,3,2,1,0,5,4:T(4,128)(2,1)S(1)}, u32[]{:S(2)}, u32[]{:S(2)}) collective-permute-start(bf16[2,6,4,4,1,1,128]{6,3,2,1,0,5,4:T(4,128)(2,1)} %get-tuple-element.166), channel_id=1, source_target_pairs={{4,0},{8,4},{12,8},{5,1},{9,5},{13,9},{6,2},{10,6},{14,10},{7,3},{... | collective-permute-start | bytes 147464 | tf_op jit(solution)/shard_map/ppermute | solution.py:21
  117.6 10.7 %all-to-all-start.2 = ((bf16[4,4,384]{2,1,0:T(4,128)(2,1)}), bf16[4,4,384]{2,1,0:T(4,128)(2,1)S(1)}, u32[]{:S(2)}, u32[]{:S(2)}) async-start(bf16[4,4,384]{2,1,0:T(4,128)(2,1)} %copy.301), calls=%async_computation.2 | async-start | bytes 24576 | tf_op jit(solution)/shard_map/all_to_all | solution.py:155
  137.1 8.6 %collective-permute-start.16 = (bf16[2,6,4,4,1,1,128]{6,3,2,1,0,5,4:T(4,128)(2,1)S(1)}, bf16[2,6,4,4,1,1,128]{6,3,2,1,0,5,4:T(4,128)(2,1)S(1)}, u32[]{:S(2)}, u32[]{:S(2)}) collective-permute-start(bf16[2,6,4,4,1,1,128]{6,3,2,1,0,5,4:T(4,128)(2,1)S(1)} %get-tuple-element.157), channel_id=1, source_target_pairs={{0,16},{1,17},{2,18},{3,19},{4,20},{5,21},{6,22},{7,23},{8,24},{9,... | collective-permute-start | bytes 147464 | tf_op jit(solution)/shard_map/ppermute | solution.py:20
  141.7 6.0 %collective-permute-start.17 = (bf16[2,6,4,4,1,1,128]{6,3,2,1,0,5,4:T(4,128)(2,1)S(1)}, bf16[2,6,4,4,1,1,128]{6,3,2,1,0,5,4:T(4,128)(2,1)S(1)}, u32[]{:S(2)}, u32[]{:S(2)}) collective-permute-start(bf16[2,6,4,4,1,1,128]{6,3,2,1,0,5,4:T(4,128)(2,1)S(1)} %get-tuple-element.158), channel_id=1, source_target_pairs={{16,0},{17,1},{18,2},{19,3},{20,4},{21,5},{22,6},{23,7},{24,8},{25... | collective-permute-start | bytes 147464 | tf_op jit(solution)/shard_map/ppermute | solution.py:21
  144.3 5.3 %collective-permute-start.19 = (bf16[2,6,4,4,1,1,128]{6,3,2,1,0,5,4:T(4,128)(2,1)S(1)}, bf16[2,6,4,4,1,1,128]{6,3,2,1,0,5,4:T(4,128)(2,1)S(1)}, u32[]{:S(2)}, u32[]{:S(2)}) collective-permute-start(bf16[2,6,4,4,1,1,128]{6,3,2,1,0,5,4:T(4,128)(2,1)S(1)} %get-tuple-element.156), channel_id=1, source_target_pairs={{4,0},{8,4},{12,8},{5,1},{9,5},{13,9},{6,2},{10,6},{14,10},{7,3},{... | collective-permute-start | bytes 147464 | tf_op jit(solution)/shard_map/ppermute | solution.py:21
  151.2 12.3 %collective-permute-start.20 = (bf16[2,6,4,4,1,1,128]{6,3,2,1,0,5,4:T(4,128)(2,1)S(1)}, bf16[2,6,4,4,1,1,128]{6,3,2,1,0,5,4:T(4,128)(2,1)S(1)}, u32[]{:S(2)}, u32[]{:S(2)}) collective-permute-start(bf16[2,6,4,4,1,1,128]{6,3,2,1,0,5,4:T(4,128)(2,1)S(1)} %get-tuple-element.147), channel_id=1, source_target_pairs={{0,16},{1,17},{2,18},{3,19},{4,20},{5,21},{6,22},{7,23},{8,24},{9,... | collective-permute-start | bytes 147464 | tf_op jit(solution)/shard_map/ppermute | solution.py:20
  155.7 7.8 %collective-permute-start.21 = (bf16[2,6,4,4,1,1,128]{6,3,2,1,0,5,4:T(4,128)(2,1)S(1)}, bf16[2,6,4,4,1,1,128]{6,3,2,1,0,5,4:T(4,128)(2,1)S(1)}, u32[]{:S(2)}, u32[]{:S(2)}) collective-permute-start(bf16[2,6,4,4,1,1,128]{6,3,2,1,0,5,4:T(4,128)(2,1)S(1)} %get-tuple-element.148), channel_id=1, source_target_pairs={{16,0},{17,1},{18,2},{19,3},{20,4},{21,5},{22,6},{23,7},{24,8},{25... | collective-permute-start | bytes 147464 | tf_op jit(solution)/shard_map/ppermute | solution.py:21
  157.0 6.5 %collective-permute-start.22 = (bf16[2,6,4,4,1,1,128]{6,3,2,1,0,5,4:T(4,128)(2,1)S(1)}, bf16[2,6,4,4,1,1,128]{6,3,2,1,0,5,4:T(4,128)(2,1)S(1)}, u32[]{:S(2)}, u32[]{:S(2)}) collective-permute-start(bf16[2,6,4,4,1,1,128]{6,3,2,1,0,5,4:T(4,128)(2,1)S(1)} %get-tuple-element.145), channel_id=1, source_target_pairs={{0,4},{4,8},{8,12},{1,5},{5,9},{9,13},{2,6},{6,10},{10,14},{3,7},{... | collective-permute-start | bytes 147464 | tf_op jit(solution)/shard_map/ppermute | solution.py:20
  (23 other events, 222.4 us)
where the time goes:
time: 209 us; the launch traced here: 208 us
  starting transfers between devices  70.7 us (34%)
  blocking collectives  56.4 us (27%)
  other arithmetic  28.5 us (14%)
  local copies, waits for them, and re-layouts  21.8 us (10%)
  waiting for transfers between devices  20 us (10%)
  matrix products  7.17 us (3%)
  between operations  2.87 us (1%)
    psum x2, blocking collectives, body(): summed = lax.psum(partial_loads, ('fx', 'fy'))  48.4 us
    ppermute x12, starting transfers between devices, with_halo(): before = lax.ppermute(last, axis, up)  41.3 us
    ppermute x12, starting transfers between devices, with_halo(): after = lax.ppermute(initial, axis, down)  15.5 us
    ppermute x12, waiting for transfers between devices, with_halo(): after = lax.ppermute(initial, axis, down)  13.9 us
    gather x2, local copies, waits for them, and re-layouts, body(): picked = received.reshape(-1)[columns]  10 us
    all_to_all x2, starting transfers between devices, body(): lax.all_to_all(shell_tangent.astype(jnp.bfloat16), 'st', split_axis=0, co...  9.96 us
    scatter-add x2, other arithmetic, body(): jnp.zeros((panels * SDOF * PN,), jnp.float32).at[columns].add(loads)  9.5 us
    all_to_all x1, blocking collectives, body(): lax.all_to_all(summed, 'st', split_axis=1, concat_axis=0, tiled=True)  7.97 us
  transfers between devices with their start and end apart: 27, of which 9 were waited for; matrix products, arithmetic and copies ran while one was open for 13% of the time, Pallas kernels for 0%

commit v1 on v0

--- a/solution.py
+++ b/solution.py
@@ -2,6 +2,7 @@
 import jax.numpy as jnp
 from jax import lax
 from jax.sharding import PartitionSpec as P
+from jax.lax import psum
 
 SDOF = 6
 PN = 64
@@ -180,7 +181,8 @@
         panels = received.shape[1]
         partial_loads = jnp.zeros((panels * SDOF * PN,), jnp.float32).at[columns].add(loads)
         partial_loads = partial_loads.reshape(1, panels, SDOF * PN)
-        summed = lax.psum(partial_loads, ("fx", "fy"))
+        state_next = psum(partial_loads, "fx")
+        summed = psum(state_next, "fy")
         owned = lax.all_to_all(summed, "st", split_axis=1, concat_axis=0, tiled=True)
         shell_adjoint = shell_solve(shell_adjoint_rhs - owned)
         shell_tangent = shell_solve(shell_load + shell_adjoint)

time: 209 us -> 202 us (0.967)
  blocking collectives: 56.4 us -> 46.2 us
  starting transfers between devices: 70.7 us -> 72.9 us
    psum x2 -> x4, blocking collectives: 48.4 us -> 38.2 us  [the longest x2 22 us: body(): summed = psum(state_next, 'fy')]
    ppermute x12, starting transfers between devices: 41.3 us -> 43.9 us  [with_halo(): before = lax.ppermute(last, axis, up)]
  transfers between devices with their start and end apart: 27 -> 27, of which waited for: 9 -> 9; matrix products, arithmetic and copies ran while one was open for 13% -> 14% of each run, Pallas kernels for 0% -> 0%
where the time goes in v1:
time: 202 us; the launch traced here: 200 us
  starting transfers between devices  72.9 us (36%)
  blocking collectives  46.2 us (23%)
  other arithmetic  28.5 us (14%)
  local copies, waits for them, and re-layouts  21.8 us (11%)
  waiting for transfers between devices  20.8 us (10%)
  matrix products  7.17 us (4%)
  between operations  2.87 us (1%)
    ppermute x12, starting transfers between devices, with_halo(): before = lax.ppermute(last, axis, up)  43.9 us
    psum x2, blocking collectives, body(): summed = psum(state_next, 'fy')  22 us
    psum x2, blocking collectives, body(): state_next = psum(partial_loads, 'fx')  16.2 us
    ppermute x12, starting transfers between devices, with_halo(): after = lax.ppermute(initial, axis, down)  15.5 us
    ppermute x12, waiting for transfers between devices, with_halo(): after = lax.ppermute(initial, axis, down)  14.7 us
    gather x2, local copies, waits for them, and re-layouts, body(): picked = received.reshape(-1)[columns]  10 us
    all_to_all x2, starting transfers between devices, body(): lax.all_to_all(shell_tangent.astype(jnp.bfloat16), 'st', split_axis=0, co...  9.63 us
    scatter-add x2, other arithmetic, body(): jnp.zeros((panels * SDOF * PN,), jnp.float32).at[columns].add(loads)  9.5 us
  transfers between devices with their start and end apart: 27, of which 9 were waited for; matrix products, arithmetic and copies ran while one was open for 14% of the time, Pallas kernels for 0%

profile of v1, /device:TPU:0, one launch (start us, length us, event | category | flops | bytes accessed | tf_op | source)
XLA Modules:
  0.0 200.3 jit_solution(4026703729437026718)
XLA Ops:
  0.7 5.0 %collective-permute-start = (bf16[2,6,4,4,1,1,128]{6,3,2,1,0,5,4:T(4,128)(2,1)S(1)}, bf16[2,6,4,4,1,1,128]{6,3,2,1,0,5,4:T(4,128)(2,1)S(1)}, u32[]{:S(2)}, u32[]{:S(2)}) collective-permute-start(bf16[2,6,4,4,1,1,128]{6,3,2,1,0,5,4:T(4,128)(2,1)S(1)} %get-tuple-element.197), channel_id=1, source_target_pairs={{0,16},{1,17},{2,18},{3,19},{4,20},{5,21},{6,22},{7,23},{8,24},{9,... | collective-permute-start | bytes 147464 | tf_op jit(solution)/shard_map/ppermute | solution.py:21
  11.7 4.9 %all-to-all-start = ((bf16[4,4,384]{2,1,0:T(4,128)(2,1)}), bf16[4,4,384]{2,1,0:T(4,128)(2,1)S(1)}, u32[]{:S(2)}, u32[]{:S(2)}) async-start(bf16[4,4,384]{2,1,0:T(4,128)(2,1)} %copy.260), calls=%async_computation | async-start | bytes 24576 | tf_op jit(solution)/shard_map/all_to_all | solution.py:156
  22.2 5.0 %gather_fusion = bf16[768]{0:T(1024)(128)(2,1)S(1)} fusion(bf16[6144]{0:T(1024)(128)(2,1)S(1)} %reshape.2599, s32[1024]{0:T(1024)S(1)} %pad_clamp_fusion.1), kind=kCustom, calls=%fused_computation | custom fusion | bytes 6144 | tf_op jit(solution)/shard_map/gather | solution.py:159
  31.5 4.4 %collective-permute-start.4 = (bf16[2,6,4,4,1,1,128]{6,3,2,1,0,5,4:T(4,128)(2,1)S(1)}, bf16[2,6,4,4,1,1,128]{6,3,2,1,0,5,4:T(4,128)(2,1)S(1)}, u32[]{:S(2)}, u32[]{:S(2)}) collective-permute-start(bf16[2,6,4,4,1,1,128]{6,3,2,1,0,5,4:T(4,128)(2,1)S(1)} %get-tuple-element.187), channel_id=1, source_target_pairs={{0,16},{1,17},{2,18},{3,19},{4,20},{5,21},{6,22},{7,23},{8,24},{9,... | collective-permute-start | bytes 147464 | tf_op jit(solution)/shard_map/ppermute | solution.py:21
  42.3 4.1 %collective-permute-done.7 = bf16[2,6,4,4,1,1,128]{6,3,2,1,0,5,4:T(4,128)(2,1)S(1)} collective-permute-done((bf16[2,6,4,4,1,1,128]{6,3,2,1,0,5,4:T(4,128)(2,1)S(1)}, bf16[2,6,4,4,1,1,128]{6,3,2,1,0,5,4:T(4,128)(2,1)S(1)}, u32[]{:S(2)}, u32[]{:S(2)}) %collective-permute-start.7) | collective-permute-done | bytes 49184 | tf_op jit(solution)/shard_map/ppermute | solution.py:22
  48.7 4.7 %collective-permute-start.10 = (bf16[2,6,4,4,1,1,128]{6,3,2,1,0,5,4:T(4,128)(2,1)S(1)}, bf16[2,6,4,4,1,1,128]{6,3,2,1,0,5,4:T(4,128)(2,1)S(1)}, u32[]{:S(2)}, u32[]{:S(2)}) collective-permute-start(bf16[2,6,4,4,1,1,128]{6,3,2,1,0,5,4:T(4,128)(2,1)S(1)} %get-tuple-element.175), channel_id=1, source_target_pairs={{0,4},{4,8},{8,12},{1,5},{5,9},{9,13},{2,6},{6,10},{10,14},{3,7},{... | collective-permute-start | bytes 147464 | tf_op jit(solution)/shard_map/ppermute | solution.py:21
  54.7 4.5 %collective-permute-start.8 = (bf16[2,6,4,4,1,1,128]{6,3,2,1,0,5,4:T(4,128)(2,1)S(1)}, bf16[2,6,4,4,1,1,128]{6,3,2,1,0,5,4:T(4,128)(2,1)S(1)}, u32[]{:S(2)}, u32[]{:S(2)}) collective-permute-start(bf16[2,6,4,4,1,1,128]{6,3,2,1,0,5,4:T(4,128)(2,1)S(1)} %get-tuple-element.177), channel_id=1, source_target_pairs={{0,16},{1,17},{2,18},{3,19},{4,20},{5,21},{6,22},{7,23},{8,24},{9,... | collective-permute-start | bytes 147464 | tf_op jit(solution)/shard_map/ppermute | solution.py:21
  61.2 4.4 %collective-permute-done.9 = bf16[2,6,4,4,1,1,128]{6,3,2,1,0,5,4:T(4,128)(2,1)S(1)} collective-permute-done((bf16[2,6,4,4,1,1,128]{6,3,2,1,0,5,4:T(4,128)(2,1)S(1)}, bf16[2,6,4,4,1,1,128]{6,3,2,1,0,5,4:T(4,128)(2,1)S(1)}, u32[]{:S(2)}, u32[]{:S(2)}) %collective-permute-start.9) | collective-permute-done | bytes 49184 | tf_op jit(solution)/shard_map/ppermute | solution.py:22
  75.3 4.8 %scatter_custom_fusion.1 = f32[6144]{0:T(1024)S(1)} fusion(s32[768]{0:T(1024)} %copy-done.12, f32[768]{0:T(1024)S(1)} %fusion.5, f32[]{:T(128)} %constant.129.clone.1), kind=kCustom, calls=%fused_computation.296 | custom fusion | flops 768 | bytes 25088 | tf_op jit(solution)/shard_map/scatter-add | solution.py:182
  80.0 7.0 %psum.28 = f32[1,16,384]{2,0,1:T(1,128)S(1)} all-reduce(f32[1,16,384]{2,0,1:T(1,128)S(1)} %bitcast.739), channel_id=1, replica_groups=mesh['fx'=2,'fy'=4,'st'=4] {'fx'}, use_global_device_ids=true, to_apply=%region_20.27 | all-reduce | flops 6144 | bytes 49152 | tf_op jit(solution)/shard_map/psum | solution.py:184
  87.0 10.8 %psum.29 = f32[1,16,384]{2,0,1:T(1,128)} all-reduce(f32[1,16,384]{2,0,1:T(1,128)S(1)} %psum.28), channel_id=1, replica_groups=mesh['fx'=2,'fy'=4,'st'=4] {'fy'}, use_global_device_ids=true, to_apply=%region_21.28 | all-reduce | flops 6144 | bytes 49152 | tf_op jit(solution)/shard_map/psum | solution.py:185
  97.9 3.9 %all-to-all-start.1 = ((f32[1,16,384]{2,0,1:T(1,128)}), f32[1,16,384]{2,0,1:T(1,128)}, u32[]{:S(2)}, u32[]{:S(2)}) async-start(f32[1,16,384]{2,0,1:T(1,128)} %psum.29), calls=%async_computation.1 | async-start | bytes 49152 | tf_op jit(solution)/shard_map/all_to_all | solution.py:186
  113.3 4.8 %all-to-all-start.2 = ((bf16[4,4,384]{2,1,0:T(4,128)(2,1)}), bf16[4,4,384]{2,1,0:T(4,128)(2,1)S(1)}, u32[]{:S(2)}, u32[]{:S(2)}) async-start(bf16[4,4,384]{2,1,0:T(4,128)(2,1)} %copy.301), calls=%async_computation.2 | async-start | bytes 24576 | tf_op jit(solution)/shard_map/all_to_all | solution.py:156
  119.3 4.4 %all-to-all-done.2 = bf16[4,4,384]{2,1,0:T(4,128)(2,1)S(1)} async-done(((bf16[4,4,384]{2,1,0:T(4,128)(2,1)}), bf16[4,4,384]{2,1,0:T(4,128)(2,1)S(1)}, u32[]{:S(2)}, u32[]{:S(2)}) %all-to-all-start.2) | async-done | bytes 12320 | tf_op jit(solution)/shard_map/all_to_all | solution.py:156
  123.7 5.0 %gather_fusion.2 = bf16[768]{0:T(1024)(128)(2,1)S(1)} fusion(bf16[6144]{0:T(1024)(128)(2,1)S(1)} %reshape.2612, s32[1024]{0:T(1024)S(1)} %pad_clamp_fusion.1), kind=kCustom, calls=%fused_computation.2 | custom fusion | bytes 6144 | tf_op jit(solution)/shard_map/gather | solution.py:159
  132.5 4.3 %collective-permute-start.16 = (bf16[2,6,4,4,1,1,128]{6,3,2,1,0,5,4:T(4,128)(2,1)S(1)}, bf16[2,6,4,4,1,1,128]{6,3,2,1,0,5,4:T(4,128)(2,1)S(1)}, u32[]{:S(2)}, u32[]{:S(2)}) collective-permute-start(bf16[2,6,4,4,1,1,128]{6,3,2,1,0,5,4:T(4,128)(2,1)S(1)} %get-tuple-element.157), channel_id=1, source_target_pairs={{0,16},{1,17},{2,18},{3,19},{4,20},{5,21},{6,22},{7,23},{8,24},{9,... | collective-permute-start | bytes 147464 | tf_op jit(solution)/shard_map/ppermute | solution.py:21
  138.1 3.2 %collective-permute-start.18 = (bf16[2,6,4,4,1,1,128]{6,3,2,1,0,5,4:T(4,128)(2,1)S(1)}, bf16[2,6,4,4,1,1,128]{6,3,2,1,0,5,4:T(4,128)(2,1)S(1)}, u32[]{:S(2)}, u32[]{:S(2)}) collective-permute-start(bf16[2,6,4,4,1,1,128]{6,3,2,1,0,5,4:T(4,128)(2,1)S(1)} %get-tuple-element.155), channel_id=1, source_target_pairs={{0,4},{4,8},{8,12},{1,5},{5,9},{9,13},{2,6},{6,10},{10,14},{3,7},{... | collective-permute-start | bytes 147464 | tf_op jit(solution)/shard_map/ppermute | solution.py:21
  143.0 4.3 %collective-permute-done.19 = bf16[2,6,4,4,1,1,128]{6,3,2,1,0,5,4:T(4,128)(2,1)S(1)} collective-permute-done((bf16[2,6,4,4,1,1,128]{6,3,2,1,0,5,4:T(4,128)(2,1)S(1)}, bf16[2,6,4,4,1,1,128]{6,3,2,1,0,5,4:T(4,128)(2,1)S(1)}, u32[]{:S(2)}, u32[]{:S(2)}) %collective-permute-start.19) | collective-permute-done | bytes 49184 | tf_op jit(solution)/shard_map/ppermute | solution.py:22
  148.9 4.5 %collective-permute-start.20 = (bf16[2,6,4,4,1,1,128]{6,3,2,1,0,5,4:T(4,128)(2,1)S(1)}, bf16[2,6,4,4,1,1,128]{6,3,2,1,0,5,4:T(4,128)(2,1)S(1)}, u32[]{:S(2)}, u32[]{:S(2)}) collective-permute-start(bf16[2,6,4,4,1,1,128]{6,3,2,1,0,5,4:T(4,128)(2,1)S(1)} %get-tuple-element.147), channel_id=1, source_target_pairs={{0,16},{1,17},{2,18},{3,19},{4,20},{5,21},{6,22},{7,23},{8,24},{9,... | collective-permute-start | bytes 147464 | tf_op jit(solution)/shard_map/ppermute | solution.py:21
  154.8 4.4 %collective-permute-start.22 = (bf16[2,6,4,4,1,1,128]{6,3,2,1,0,5,4:T(4,128)(2,1)S(1)}, bf16[2,6,4,4,1,1,128]{6,3,2,1,0,5,4:T(4,128)(2,1)S(1)}, u32[]{:S(2)}, u32[]{:S(2)}) collective-permute-start(bf16[2,6,4,4,1,1,128]{6,3,2,1,0,5,4:T(4,128)(2,1)S(1)} %get-tuple-element.145), channel_id=1, source_target_pairs={{0,4},{4,8},{8,12},{1,5},{5,9},{9,13},{2,6},{6,10},{10,14},{3,7},{... | collective-permute-start | bytes 147464 | tf_op jit(solution)/shard_map/ppermute | solution.py:21
  165.0 4.8 %scatter_custom_fusion.3 = f32[6144]{0:T(1024)S(1)} fusion(s32[768]{0:T(1024)} %copy-done.12, f32[768]{0:T(1024)S(1)} %fusion.4, f32[]{:T(128)} %constant.129.clone.1), kind=kCustom, calls=%fused_computation.294 | custom fusion | flops 768 | bytes 25088 | tf_op jit(solution)/shard_map/scatter-add | solution.py:182
  169.8 9.2 %psum.30 = f32[1,16,384]{2,0,1:T(1,128)S(1)} all-reduce(f32[1,16,384]{2,0,1:T(1,128)S(1)} %bitcast.738), channel_id=1, replica_groups=mesh['fx'=2,'fy'=4,'st'=4] {'fx'}, use_global_device_ids=true, to_apply=%region_42.49 | all-reduce | flops 6144 | bytes 49152 | tf_op jit(solution)/shard_map/psum | solution.py:184
  179.0 11.1 %psum.31 = f32[1,16,384]{2,0,1:T(1,128)S(1)} all-reduce(f32[1,16,384]{2,0,1:T(1,128)S(1)} %psum.30), channel_id=1, replica_groups=mesh['fx'=2,'fy'=4,'st'=4] {'fy'}, use_global_device_ids=true, to_apply=%region_43.50 | all-reduce | flops 6144 | bytes 49152 | tf_op jit(solution)/shard_map/psum | solution.py:185
  190.1 8.0 %all_to_all.42 = f32[1,16,384]{2,0,1:T(1,128)S(1)} all-to-all(f32[1,16,384]{2,0,1:T(1,128)S(1)} %psum.31), channel_id=1, replica_groups=mesh['fx'=2,'fy'=4,'st'=4] {'st'}, dimensions={1} | all-to-all | bytes 49152 | tf_op jit(solution)/shard_map/all_to_all | solution.py:186
  (266 shorter events, 66.0 us)
Async XLA Ops:
  0.7 28.4 %collective-permute-start = (bf16[2,6,4,4,1,1,128]{6,3,2,1,0,5,4:T(4,128)(2,1)S(1)}, bf16[2,6,4,4,1,1,128]{6,3,2,1,0,5,4:T(4,128)(2,1)S(1)}, u32[]{:S(2)}, u32[]{:S(2)}) collective-permute-start(bf16[2,6,4,4,1,1,128]{6,3,2,1,0,5,4:T(4,128)(2,1)S(1)} %get-tuple-element.197), channel_id=1, source_target_pairs={{0,16},{1,17},{2,18},{3,19},{4,20},{5,21},{6,22},{7,23},{8,24},{9,... | collective-permute-start | bytes 147464 | tf_op jit(solution)/shard_map/ppermute | solution.py:21
  5.8 23.3 %collective-permute-start.1 = (bf16[2,6,4,4,1,1,128]{6,3,2,1,0,5,4:T(4,128)(2,1)S(1)}, bf16[2,6,4,4,1,1,128]{6,3,2,1,0,5,4:T(4,128)(2,1)S(1)}, u32[]{:S(2)}, u32[]{:S(2)}) collective-permute-start(bf16[2,6,4,4,1,1,128]{6,3,2,1,0,5,4:T(4,128)(2,1)S(1)} %get-tuple-element.198), channel_id=1, source_target_pairs={{16,0},{17,1},{18,2},{19,3},{20,4},{21,5},{22,6},{23,7},{24,8},{25... | collective-permute-start | bytes 147464 | tf_op jit(solution)/shard_map/ppermute | solution.py:22
  7.1 22.0 %collective-permute-start.2 = (bf16[2,6,4,4,1,1,128]{6,3,2,1,0,5,4:T(4,128)(2,1)S(1)}, bf16[2,6,4,4,1,1,128]{6,3,2,1,0,5,4:T(4,128)(2,1)S(1)}, u32[]{:S(2)}, u32[]{:S(2)}) collective-permute-start(bf16[2,6,4,4,1,1,128]{6,3,2,1,0,5,4:T(4,128)(2,1)S(1)} %get-tuple-element.195), channel_id=1, source_target_pairs={{0,4},{4,8},{8,12},{1,5},{5,9},{9,13},{2,6},{6,10},{10,14},{3,7},{... | collective-permute-start | bytes 147464 | tf_op jit(solution)/shard_map/ppermute | solution.py:21
  8.6 20.5 %collective-permute-start.3 = (bf16[2,6,4,4,1,1,128]{6,3,2,1,0,5,4:T(4,128)(2,1)S(1)}, bf16[2,6,4,4,1,1,128]{6,3,2,1,0,5,4:T(4,128)(2,1)S(1)}, u32[]{:S(2)}, u32[]{:S(2)}) collective-permute-start(bf16[2,6,4,4,1,1,128]{6,3,2,1,0,5,4:T(4,128)(2,1)S(1)} %get-tuple-element.196), channel_id=1, source_target_pairs={{4,0},{8,4},{12,8},{5,1},{9,5},{13,9},{6,2},{10,6},{14,10},{7,3},{... | collective-permute-start | bytes 147464 | tf_op jit(solution)/shard_map/ppermute | solution.py:22
  11.7 10.5 %all-to-all-start = ((bf16[4,4,384]{2,1,0:T(4,128)(2,1)}), bf16[4,4,384]{2,1,0:T(4,128)(2,1)S(1)}, u32[]{:S(2)}, u32[]{:S(2)}) async-start(bf16[4,4,384]{2,1,0:T(4,128)(2,1)} %copy.260), calls=%async_computation | async-start | bytes 24576 | tf_op jit(solution)/shard_map/all_to_all | solution.py:156
  31.5 10.2 %collective-permute-start.4 = (bf16[2,6,4,4,1,1,128]{6,3,2,1,0,5,4:T(4,128)(2,1)S(1)}, bf16[2,6,4,4,1,1,128]{6,3,2,1,0,5,4:T(4,128)(2,1)S(1)}, u32[]{:S(2)}, u32[]{:S(2)}) collective-permute-start(bf16[2,6,4,4,1,1,128]{6,3,2,1,0,5,4:T(4,128)(2,1)S(1)} %get-tuple-element.187), channel_id=1, source_target_pairs={{0,16},{1,17},{2,18},{3,19},{4,20},{5,21},{6,22},{7,23},{8,24},{9,... | collective-permute-start | bytes 147464 | tf_op jit(solution)/shard_map/ppermute | solution.py:21
  35.9 6.3 %collective-permute-start.5 = (bf16[2,6,4,4,1,1,128]{6,3,2,1,0,5,4:T(4,128)(2,1)S(1)}, bf16[2,6,4,4,1,1,128]{6,3,2,1,0,5,4:T(4,128)(2,1)S(1)}, u32[]{:S(2)}, u32[]{:S(2)}) collective-permute-start(bf16[2,6,4,4,1,1,128]{6,3,2,1,0,5,4:T(4,128)(2,1)S(1)} %get-tuple-element.188), channel_id=1, source_target_pairs={{16,0},{17,1},{18,2},{19,3},{20,4},{21,5},{22,6},{23,7},{24,8},{25... | collective-permute-start | bytes 147464 | tf_op jit(solution)/shard_map/ppermute | solution.py:22
  40.3 6.1 %collective-permute-start.7 = (bf16[2,6,4,4,1,1,128]{6,3,2,1,0,5,4:T(4,128)(2,1)S(1)}, bf16[2,6,4,4,1,1,128]{6,3,2,1,0,5,4:T(4,128)(2,1)S(1)}, u32[]{:S(2)}, u32[]{:S(2)}) collective-permute-start(bf16[2,6,4,4,1,1,128]{6,3,2,1,0,5,4:T(4,128)(2,1)S(1)} %get-tuple-element.186), channel_id=1, source_target_pairs={{4,0},{8,4},{12,8},{5,1},{9,5},{13,9},{6,2},{10,6},{14,10},{7,3},{... | collective-permute-start | bytes 147464 | tf_op jit(solution)/shard_map/ppermute | solution.py:22
  48.7 12.0 %collective-permute-start.10 = (bf16[2,6,4,4,1,1,128]{6,3,2,1,0,5,4:T(4,128)(2,1)S(1)}, bf16[2,6,4,4,1,1,128]{6,3,2,1,0,5,4:T(4,128)(2,1)S(1)}, u32[]{:S(2)}, u32[]{:S(2)}) collective-permute-start(bf16[2,6,4,4,1,1,128]{6,3,2,1,0,5,4:T(4,128)(2,1)S(1)} %get-tuple-element.175), channel_id=1, source_target_pairs={{0,4},{4,8},{8,12},{1,5},{5,9},{9,13},{2,6},{6,10},{10,14},{3,7},{... | collective-permute-start | bytes 147464 | tf_op jit(solution)/shard_map/ppermute | solution.py:21
  53.4 7.3 %collective-permute-start.11 = (bf16[2,6,4,4,1,1,128]{6,3,2,1,0,5,4:T(4,128)(2,1)S(1)}, bf16[2,6,4,4,1,1,128]{6,3,2,1,0,5,4:T(4,128)(2,1)S(1)}, u32[]{:S(2)}, u32[]{:S(2)}) collective-permute-start(bf16[2,6,4,4,1,1,128]{6,3,2,1,0,5,4:T(4,128)(2,1)S(1)} %get-tuple-element.176), channel_id=1, source_target_pairs={{4,0},{8,4},{12,8},{5,1},{9,5},{13,9},{6,2},{10,6},{14,10},{7,3},{... | collective-permute-start | bytes 147464 | tf_op jit(solution)/shard_map/ppermute | solution.py:22
  54.7 6.5 %collective-permute-start.8 = (bf16[2,6,4,4,1,1,128]{6,3,2,1,0,5,4:T(4,128)(2,1)S(1)}, bf16[2,6,4,4,1,1,128]{6,3,2,1,0,5,4:T(4,128)(2,1)S(1)}, u32[]{:S(2)}, u32[]{:S(2)}) collective-permute-start(bf16[2,6,4,4,1,1,128]{6,3,2,1,0,5,4:T(4,128)(2,1)S(1)} %get-tuple-element.177), channel_id=1, source_target_pairs={{0,16},{1,17},{2,18},{3,19},{4,20},{5,21},{6,22},{7,23},{8,24},{9,... | collective-permute-start | bytes 147464 | tf_op jit(solution)/shard_map/ppermute | solution.py:21
  59.3 6.4 %collective-permute-start.9 = (bf16[2,6,4,4,1,1,128]{6,3,2,1,0,5,4:T(4,128)(2,1)S(1)}, bf16[2,6,4,4,1,1,128]{6,3,2,1,0,5,4:T(4,128)(2,1)S(1)}, u32[]{:S(2)}, u32[]{:S(2)}) collective-permute-start(bf16[2,6,4,4,1,1,128]{6,3,2,1,0,5,4:T(4,128)(2,1)S(1)} %get-tuple-element.178), channel_id=1, source_target_pairs={{16,0},{17,1},{18,2},{19,3},{20,4},{21,5},{22,6},{23,7},{24,8},{25... | collective-permute-start | bytes 147464 | tf_op jit(solution)/shard_map/ppermute | solution.py:22
  71.2 46.9 %collective-permute-start.12 = (bf16[2,6,4,4,1,1,128]{6,3,2,1,0,5,4:T(4,128)(2,1)}, bf16[2,6,4,4,1,1,128]{6,3,2,1,0,5,4:T(4,128)(2,1)}, u32[]{:S(2)}, u32[]{:S(2)}) collective-permute-start(bf16[2,6,4,4,1,1,128]{6,3,2,1,0,5,4:T(4,128)(2,1)} %get-tuple-element.167), channel_id=1, source_target_pairs={{0,16},{1,17},{2,18},{3,19},{4,20},{5,21},{6,22},{7,23},{8,24},{9,... | collective-permute-start | bytes 147464 | tf_op jit(solution)/shard_map/ppermute | solution.py:21
  97.9 11.7 %all-to-all-start.1 = ((f32[1,16,384]{2,0,1:T(1,128)}), f32[1,16,384]{2,0,1:T(1,128)}, u32[]{:S(2)}, u32[]{:S(2)}) async-start(f32[1,16,384]{2,0,1:T(1,128)} %psum.29), calls=%async_computation.1 | async-start | bytes 49152 | tf_op jit(solution)/shard_map/all_to_all | solution.py:186
  104.7 13.4 %collective-permute-start.13 = (bf16[2,6,4,4,1,1,128]{6,3,2,1,0,5,4:T(4,128)(2,1)}, bf16[2,6,4,4,1,1,128]{6,3,2,1,0,5,4:T(4,128)(2,1)S(1)}, u32[]{:S(2)}, u32[]{:S(2)}) collective-permute-start(bf16[2,6,4,4,1,1,128]{6,3,2,1,0,5,4:T(4,128)(2,1)} %get-tuple-element.168), channel_id=1, source_target_pairs={{16,0},{17,1},{18,2},{19,3},{20,4},{21,5},{22,6},{23,7},{24,8},{25... | collective-permute-start | bytes 147464 | tf_op jit(solution)/shard_map/ppermute | solution.py:22
  106.0 12.1 %collective-permute-start.14 = (bf16[2,6,4,4,1,1,128]{6,3,2,1,0,5,4:T(4,128)(2,1)}, bf16[2,6,4,4,1,1,128]{6,3,2,1,0,5,4:T(4,128)(2,1)S(1)}, u32[]{:S(2)}, u32[]{:S(2)}) collective-permute-start(bf16[2,6,4,4,1,1,128]{6,3,2,1,0,5,4:T(4,128)(2,1)} %get-tuple-element.165), channel_id=1, source_target_pairs={{0,4},{4,8},{8,12},{1,5},{5,9},{9,13},{2,6},{6,10},{10,14},{3,7},{... | collective-permute-start | bytes 147464 | tf_op jit(solution)/shard_map/ppermute | solution.py:21
  108.3 9.8 %collective-permute-start.15 = (bf16[2,6,4,4,1,1,128]{6,3,2,1,0,5,4:T(4,128)(2,1)}, bf16[2,6,4,4,1,1,128]{6,3,2,1,0,5,4:T(4,128)(2,1)S(1)}, u32[]{:S(2)}, u32[]{:S(2)}) collective-permute-start(bf16[2,6,4,4,1,1,128]{6,3,2,1,0,5,4:T(4,128)(2,1)} %get-tuple-element.166), channel_id=1, source_target_pairs={{4,0},{8,4},{12,8},{5,1},{9,5},{13,9},{6,2},{10,6},{14,10},{7,3},{... | collective-permute-start | bytes 147464 | tf_op jit(solution)/shard_map/ppermute | solution.py:22
  113.3 10.4 %all-to-all-start.2 = ((bf16[4,4,384]{2,1,0:T(4,128)(2,1)}), bf16[4,4,384]{2,1,0:T(4,128)(2,1)S(1)}, u32[]{:S(2)}, u32[]{:S(2)}) async-start(bf16[4,4,384]{2,1,0:T(4,128)(2,1)} %copy.301), calls=%async_computation.2 | async-start | bytes 24576 | tf_op jit(solution)/shard_map/all_to_all | solution.py:156
  132.5 10.2 %collective-permute-start.16 = (bf16[2,6,4,4,1,1,128]{6,3,2,1,0,5,4:T(4,128)(2,1)S(1)}, bf16[2,6,4,4,1,1,128]{6,3,2,1,0,5,4:T(4,128)(2,1)S(1)}, u32[]{:S(2)}, u32[]{:S(2)}) collective-permute-start(bf16[2,6,4,4,1,1,128]{6,3,2,1,0,5,4:T(4,128)(2,1)S(1)} %get-tuple-element.157), channel_id=1, source_target_pairs={{0,16},{1,17},{2,18},{3,19},{4,20},{5,21},{6,22},{7,23},{8,24},{9,... | collective-permute-start | bytes 147464 | tf_op jit(solution)/shard_map/ppermute | solution.py:21
  136.8 6.2 %collective-permute-start.17 = (bf16[2,6,4,4,1,1,128]{6,3,2,1,0,5,4:T(4,128)(2,1)S(1)}, bf16[2,6,4,4,1,1,128]{6,3,2,1,0,5,4:T(4,128)(2,1)S(1)}, u32[]{:S(2)}, u32[]{:S(2)}) collective-permute-start(bf16[2,6,4,4,1,1,128]{6,3,2,1,0,5,4:T(4,128)(2,1)S(1)} %get-tuple-element.158), channel_id=1, source_target_pairs={{16,0},{17,1},{18,2},{19,3},{20,4},{21,5},{22,6},{23,7},{24,8},{25... | collective-permute-start | bytes 147464 | tf_op jit(solution)/shard_map/ppermute | solution.py:22
  141.2 6.1 %collective-permute-start.19 = (bf16[2,6,4,4,1,1,128]{6,3,2,1,0,5,4:T(4,128)(2,1)S(1)}, bf16[2,6,4,4,1,1,128]{6,3,2,1,0,5,4:T(4,128)(2,1)S(1)}, u32[]{:S(2)}, u32[]{:S(2)}) collective-permute-start(bf16[2,6,4,4,1,1,128]{6,3,2,1,0,5,4:T(4,128)(2,1)S(1)} %get-tuple-element.156), channel_id=1, source_target_pairs={{4,0},{8,4},{12,8},{5,1},{9,5},{13,9},{6,2},{10,6},{14,10},{7,3},{... | collective-permute-start | bytes 147464 | tf_op jit(solution)/shard_map/ppermute | solution.py:22
  148.9 12.3 %collective-permute-start.20 = (bf16[2,6,4,4,1,1,128]{6,3,2,1,0,5,4:T(4,128)(2,1)S(1)}, bf16[2,6,4,4,1,1,128]{6,3,2,1,0,5,4:T(4,128)(2,1)S(1)}, u32[]{:S(2)}, u32[]{:S(2)}) collective-permute-start(bf16[2,6,4,4,1,1,128]{6,3,2,1,0,5,4:T(4,128)(2,1)S(1)} %get-tuple-element.147), channel_id=1, source_target_pairs={{0,16},{1,17},{2,18},{3,19},{4,20},{5,21},{6,22},{7,23},{8,24},{9,... | collective-permute-start | bytes 147464 | tf_op jit(solution)/shard_map/ppermute | solution.py:21
  153.5 7.8 %collective-permute-start.21 = (bf16[2,6,4,4,1,1,128]{6,3,2,1,0,5,4:T(4,128)(2,1)S(1)}, bf16[2,6,4,4,1,1,128]{6,3,2,1,0,5,4:T(4,128)(2,1)S(1)}, u32[]{:S(2)}, u32[]{:S(2)}) collective-permute-start(bf16[2,6,4,4,1,1,128]{6,3,2,1,0,5,4:T(4,128)(2,1)S(1)} %get-tuple-element.148), channel_id=1, source_target_pairs={{16,0},{17,1},{18,2},{19,3},{20,4},{21,5},{22,6},{23,7},{24,8},{25... | collective-permute-start | bytes 147464 | tf_op jit(solution)/shard_map/ppermute | solution.py:22
  154.8 6.5 %collective-permute-start.22 = (bf16[2,6,4,4,1,1,128]{6,3,2,1,0,5,4:T(4,128)(2,1)S(1)}, bf16[2,6,4,4,1,1,128]{6,3,2,1,0,5,4:T(4,128)(2,1)S(1)}, u32[]{:S(2)}, u32[]{:S(2)}) collective-permute-start(bf16[2,6,4,4,1,1,128]{6,3,2,1,0,5,4:T(4,128)(2,1)S(1)} %get-tuple-element.145), channel_id=1, source_target_pairs={{0,4},{4,8},{8,12},{1,5},{5,9},{9,13},{2,6},{6,10},{10,14},{3,7},{... | collective-permute-start | bytes 147464 | tf_op jit(solution)/shard_map/ppermute | solution.py:21
  (23 other events, 207.4 us)
